TPU v7x, 256 devices: a whole 4x4x8 slice. The times are simulated.
256 devices in a mesh: seq: 8 (over z), head: 32 (over y, x, core).
Axes of the slice: x: 4, y: 4, z: 8, core: 2. Of those that a mesh axis runs over, the one named last changes fastest.
Arguments:
- queries: bfloat16 [4096, 32, 128], P(('seq', 'head')), may hold values from -6 to 6
- keys: bfloat16 [4096, 32, 128], P(('seq', 'head')), may hold values from -6 to 6
- values: bfloat16 [4096, 32, 128], P(('seq', 'head')), may hold values from -6 to 6
- out_grad: bfloat16 [4096, 32, 128], P(('seq', 'head')), may hold values from -1.5 to 1.5
- level_weights: float32 [32, 13, 4096], P('head', None, 'seq'), may hold values from 0.2 to 2
Outputs:
- query_grad: bfloat16 [4096, 32, 128], P(('seq', 'head'))
- key_grad: bfloat16 [4096, 32, 128], P(('seq', 'head'))
- value_grad: bfloat16 [4096, 32, 128], P(('seq', 'head'))
- weight_grad: float32 [32, 13, 4096], P('head', None, 'seq')
All inputs are finite; a program needn't handle non-finite values.
Results may differ from a plain program's by a relative error of at most 0.0052.
Values may be sent and summed in bfloat16 or wider, within the bound.
No kernel may reach another device: no remote copies, remote signals or barrier semaphores. Data moves between devices by JAX's collectives and lax.ppermute only.
A program may use at most 64 MiB of HBM per device.

v0:
```python
import math
import jax
import jax.numpy as jnp
from jax import lax
from jax.sharding import PartitionSpec as P


def partner(value, axis, apart):
    mask = 2**apart
    pairs = [(source, source ^ mask) for source in range(lax.axis_size(axis))]
    return lax.ppermute(value, axis, pairs)


def bit_length(values, number):
    running = jnp.zeros(values.shape, jnp.int32)
    for exponent in range(number):
        running = running + (values >= 2**exponent).astype(jnp.int32)
    return running


def level_factor(degree, head_width):
    base_scale = 1.0 / math.sqrt(head_width)
    if degree == 0:
        return base_scale
    return base_scale * 2.0 ** (-(degree - 1) / 2.0)


def spread_states(lower_source, upper_source):
    far_count = lax.axis_size("seq").bit_length() - 1
    position = lax.axis_index("seq")
    lower_states = []
    upper_states = []
    offset = 1
    running = lower_source
    pending = list(upper_source)
    for degree in range(far_count):
        outgoing = [running] + pending[degree:]
        received = partner(jnp.stack(outgoing), "seq", degree)
        upper_bit = position // 2**degree % 2 == 1
        lower_states.append(jnp.where(upper_bit, received[0], 0.0))
        running = running + received[0]
        upper_states.append(jnp.where(upper_bit, 0.0, received[offset]))
        for later_level in range(degree + 1, far_count):
            pending[later_level] = pending[later_level] + received[offset + later_level - degree]
    return (lower_states, upper_states)


def query_states(query_rows, grad_rows, level_weights, first_far):
    head_width = query_rows.shape[2]
    far_count = level_weights.shape[1] - first_far
    coefficients = jnp.stack(
        [
            level_factor(first_far + degree, head_width) * level_weights[:, first_far + degree, :]
            for degree in range(far_count)
        ]
    )
    scaled = (jnp.transpose(coefficients, (0, 2, 1))[..., None] * grad_rows[None]).astype(
        jnp.bfloat16
    )
    states = jnp.einsum("thd,jthe->jhde", query_rows, scaled, preferred_element_type=jnp.float32)
    return (coefficients, [states[degree] for degree in range(far_count)])


def near_terms(query_rows, key_rows, value_rows, grad_rows, level_weights):
    tok_count = query_rows.shape[0]
    heads_here = query_rows.shape[1]
    head_width = query_rows.shape[2]
    block_rows = min(512, tok_count)
    block_bits = block_rows.bit_length() - 1
    local_bits = tok_count.bit_length() - 1
    pieces = tok_count // block_rows
    zero_block = jnp.zeros((block_rows, heads_here, head_width), jnp.float32)
    zero_weights = jnp.zeros((heads_here, block_rows), jnp.float32)
    query_parts = [zero_block] * pieces
    key_parts = [zero_block] * pieces
    value_parts = [zero_block] * pieces
    weight_rows = [[zero_weights] * pieces for degree in range(local_bits + 1)]
    positions = jnp.arange(block_rows, dtype=jnp.int32)
    crossed = jnp.bitwise_xor(positions[:, None], positions[None, :])
    causal = positions[None, :] <= positions[:, None]
    inside = bit_length(crossed, block_bits)
    scores = jnp.einsum("thd,shd->hts", query_rows, key_rows, preferred_element_type=jnp.float32)
    pulls = jnp.einsum("the,she->hts", grad_rows, value_rows, preferred_element_type=jnp.float32)
    product = jnp.where(causal[None], scores * pulls, 0.0)
    weights = jnp.zeros(scores.shape, jnp.float32)
    for degree in range(block_bits + 1):
        factor = level_factor(degree, head_width)
        matching = (causal & (inside == degree))[None]
        column = (factor * level_weights[:, degree, :])[:, :, None]
        weights = jnp.where(matching, column, weights)
        chosen = jnp.sum(jnp.where(matching, product, 0.0), axis=2)
        weight_rows[degree][0] = factor * chosen
    near_scaled = (weights * scores).astype(jnp.bfloat16)
    near_pulled = (weights * pulls).astype(jnp.bfloat16)
    value_parts[0] = jnp.einsum(
        "hts,the->she", near_scaled, grad_rows, preferred_element_type=jnp.float32
    )
    query_parts[0] = jnp.einsum(
        "hts,shd->thd", near_pulled, key_rows, preferred_element_type=jnp.float32
    )
    key_parts[0] = jnp.einsum(
        "hts,thd->shd", near_pulled, query_rows, preferred_element_type=jnp.float32
    )
    weight_near = [jnp.concatenate(weight_rows[degree], axis=1) for degree in range(local_bits + 1)]
    return (query_parts[0], key_parts[0], value_parts[0], weight_near)


def on_device(queries, keys, values, out_grad, level_weights):
    query_rows, key_rows, value_rows, grad_rows = (
        lax.all_to_all(queries, "head", split_axis=1, concat_axis=0, tiled=True),
        lax.all_to_all(keys, "head", split_axis=1, concat_axis=0, tiled=True),
        lax.all_to_all(values, "head", split_axis=1, concat_axis=0, tiled=True),
        lax.all_to_all(out_grad, "head", split_axis=1, concat_axis=0, tiled=True),
    )
    first_far = query_rows.shape[0].bit_length()
    key_state = jnp.einsum("shd,she->hde", key_rows, value_rows, preferred_element_type=jnp.float32)
    coefficients, upper_parts = query_states(query_rows, grad_rows, level_weights, first_far)
    lower_states, upper_states = spread_states(key_state, upper_parts)
    head_width = query_rows.shape[2]
    far_count = level_weights.shape[1] - first_far
    query_near, key_near, value_near, weight_near = near_terms(
        query_rows, key_rows, value_rows, grad_rows, level_weights
    )
    lower_narrow = jnp.stack([matrix.astype(jnp.bfloat16) for matrix in lower_states])
    far_update = jnp.einsum(
        "the,jhde->jthd", grad_rows, lower_narrow, preferred_element_type=jnp.float32
    )
    query_total = query_near + jnp.sum(
        jnp.transpose(coefficients, (0, 2, 1))[..., None] * far_update, axis=0
    )
    upper_total = upper_states[0]
    for degree in range(1, far_count):
        upper_total = upper_total + upper_states[degree]
    upper_narrow = upper_total.astype(jnp.bfloat16)
    key_total = key_near + jnp.einsum(
        "she,hde->shd", value_rows, upper_narrow, preferred_element_type=jnp.float32
    )
    value_total = value_near + jnp.einsum(
        "shd,hde->she", key_rows, upper_narrow, preferred_element_type=jnp.float32
    )
    factors = jnp.array(
        [level_factor(first_far + degree, head_width) for degree in range(far_count)], jnp.float32
    )
    weight_far = factors[:, None, None] * jnp.sum(query_rows[None] * far_update, axis=-1)
    weight_grad = jnp.stack(
        weight_near + [weight_far[degree].T for degree in range(far_count)], axis=1
    )
    query_out, key_out, value_out = (
        lax.all_to_all(
            query_total.astype(jnp.bfloat16), "head", split_axis=0, concat_axis=1, tiled=True
        ),
        lax.all_to_all(
            key_total.astype(jnp.bfloat16), "head", split_axis=0, concat_axis=1, tiled=True
        ),
        lax.all_to_all(
            value_total.astype(jnp.bfloat16), "head", split_axis=0, concat_axis=1, tiled=True
        ),
    )
    return (query_out, key_out, value_out, weight_grad)


def solution(mesh):
    in_specs = (
        P(("seq", "head"), None, None),
        P(("seq", "head"), None, None),
        P(("seq", "head"), None, None),
        P(("seq", "head"), None, None),
        P("head", None, "seq"),
    )
    out_specs = (
        P(("seq", "head"), None, None),
        P(("seq", "head"), None, None),
        P(("seq", "head"), None, None),
        P("head", None, "seq"),
    )
    return jax.shard_map(
        on_device, mesh=mesh, in_specs=in_specs, out_specs=out_specs, check_vma=False
    )
```

profile of v0, /device:TPU:1, one launch (start us, length us, event | category | flops | bytes accessed | tf_op | source)
XLA Modules:
  0.0 130.0 jit_solution(8321953172399653575)
XLA Ops:
  0.6 1.6 %copy.54 = bf16[16,32,128]{2,0,1:T(8,128)(2,1)} copy(bf16[16,32,128]{2,1,0:T(8,128)(2,1)} %param.9) | data formatting | bytes 262144 | tf_op args[3]
  2.2 8.7 %all-to-all-start = ((bf16[16,32,128]{2,0,1:T(8,128)(2,1)}), bf16[16,32,128]{2,0,1:T(8,128)(2,1)S(1)}, u32[]{:S(2)}, u32[]{:S(2)}) async-start(bf16[16,32,128]{2,0,1:T(8,128)(2,1)} %copy.54), calls=%async_computation | async-start | bytes 262144 | tf_op jit(solution)/shard_map/all_to_all | solution.py:113
  11.0 0.7 copy.55
  11.7 6.9 %all-to-all-done = bf16[16,32,128]{2,0,1:T(8,128)(2,1)S(1)} async-done(((bf16[16,32,128]{2,0,1:T(8,128)(2,1)}), bf16[16,32,128]{2,0,1:T(8,128)(2,1)S(1)}, u32[]{:S(2)}, u32[]{:S(2)}) %all-to-all-start) | async-done | bytes 131104 | tf_op jit(solution)/shard_map/all_to_all | solution.py:113
  18.6 3.9 %all-to-all-start.1 = ((bf16[16,32,128]{2,0,1:T(8,128)(2,1)}), bf16[16,32,128]{2,0,1:T(8,128)(2,1)S(1)}, u32[]{:S(2)}, u32[]{:S(2)}) async-start(bf16[16,32,128]{2,0,1:T(8,128)(2,1)} %copy.55), calls=%async_computation.1 | async-start | bytes 262144 | tf_op jit(solution)/shard_map/all_to_all | solution.py:112
  22.5 0.7 copy.58
  23.2 7.0 %all-to-all-done.1 = bf16[16,32,128]{2,0,1:T(8,128)(2,1)S(1)} async-done(((bf16[16,32,128]{2,0,1:T(8,128)(2,1)}), bf16[16,32,128]{2,0,1:T(8,128)(2,1)S(1)}, u32[]{:S(2)}, u32[]{:S(2)}) %all-to-all-start.1) | async-done | bytes 131104 | tf_op jit(solution)/shard_map/all_to_all | solution.py:112
  30.2 3.9 %all-to-all-start.2 = ((bf16[16,32,128]{2,0,1:T(8,128)(2,1)}), bf16[16,32,128]{2,0,1:T(8,128)(2,1)S(1)}, u32[]{:S(2)}, u32[]{:S(2)}) async-start(bf16[16,32,128]{2,0,1:T(8,128)(2,1)} %copy.58), calls=%async_computation.2 | async-start | bytes 262144 | tf_op jit(solution)/shard_map/all_to_all | solution.py:111
  34.2 0.8 copy-done.2
  35.1 0.7 copy.62
  35.9 6.0 %all-to-all-done.2 = bf16[16,32,128]{2,0,1:T(8,128)(2,1)S(1)} async-done(((bf16[16,32,128]{2,0,1:T(8,128)(2,1)}), bf16[16,32,128]{2,0,1:T(8,128)(2,1)S(1)}, u32[]{:S(2)}, u32[]{:S(2)}) %all-to-all-start.2) | async-done | bytes 131104 | tf_op jit(solution)/shard_map/all_to_all | solution.py:111
  41.8 3.9 %all-to-all-start.3 = ((bf16[16,32,128]{2,0,1:T(8,128)(2,1)}), bf16[16,32,128]{2,0,1:T(8,128)(2,1)S(1)}, u32[]{:S(2)}, u32[]{:S(2)}) async-start(bf16[16,32,128]{2,0,1:T(8,128)(2,1)} %copy.62), calls=%async_computation.3 | async-start | bytes 262144 | tf_op jit(solution)/shard_map/all_to_all | solution.py:110
  45.8 0.3 fusion.61
  46.2 7.3 %all-to-all-done.3 = bf16[16,32,128]{2,0,1:T(8,128)(2,1)S(1)} async-done(((bf16[16,32,128]{2,0,1:T(8,128)(2,1)}), bf16[16,32,128]{2,0,1:T(8,128)(2,1)S(1)}, u32[]{:S(2)}, u32[]{:S(2)}) %all-to-all-start.3) | async-done | bytes 131104 | tf_op jit(solution)/shard_map/all_to_all | solution.py:110
  53.5 1.7 %fusion.9 = (f32[512,512]{0,1:T(8,128)S(1)}, bf16[512,512]{0,1:T(8,128)(2,1)S(1)}, f32[512,512]{0,1:T(8,128)}) fusion(f32[512,512]{0,1:T(8,128)S(1)} %fusion.61, f32[512]{0:T(512)S(1)} %bitcast.184, f32[512]{0:T(512)S(1)} %bitcast.186, f32[512]{0:T(512)S(1)} %bitcast.188, f32[512]{0:T(512)S(1)} %bitcast.190, f32[512]{0:T(512)S(1)} %bitcast.192, ...), kind=kOutput, calls=%fused_computation.11 | convolution fusion | flops 83361792 | bytes 3952640 | tf_op jit(solution)/shard_map/thd,shd->hts/dot_general | solution.py:82
  55.2 3.1 %select_reduce_fusion = (f32[512]{0:T(512)S(1)}, f32[512]{0:T(512)S(1)}, f32[512]{0:T(512)S(1)}, f32[512]{0:T(512)S(1)}, f32[512]{0:T(512)S(1)}, /*index=5*/f32[...) fusion(f32[512,512]{0,1:T(8,128)S(1)} %get-tuple-element.28), kind=kLoop, calls=%fused_computation.35 | loop fusion | flops 17820672 | bytes 1069056 | tf_op jit(solution)/shard_map/reduce_sum | solution.py:91
  58.5 0.3 convolution_bitcast_fusion.4
  58.8 0.2 fusion.28
  59.1 1.7 %collective-permute-start = (f32[4,1,128,128]{3,2,1,0:T(8,128)S(1)}, f32[4,1,128,128]{3,2,1,0:T(8,128)S(1)}, u32[]{:S(2)}, u32[]{:S(2)}) collective-permute-start(f32[4,1,128,128]{3,2,1,0:T(8,128)S(1)} %pad_maximum_fusion), channel_id=1, source_target_pairs={{0,32},{32,0},{64,96},{96,64},{128,160},{160,128},{192,224},{224,1... | collective-permute-start | bytes 786440 | tf_op jit(solution)/shard_map/ppermute | solution.py:11
  60.8 0.8 convolution_bitcast_fusion.1
  61.9 0.3 convolution_bitcast_fusion.2
  62.2 4.8 %collective-permute-done = f32[4,1,128,128]{3,2,1,0:T(8,128)S(1)} collective-permute-done((f32[4,1,128,128]{3,2,1,0:T(8,128)S(1)}, f32[4,1,128,128]{3,2,1,0:T(8,128)S(1)}, u32[]{:S(2)}, u32[]{:S(2)}) %collective-permute-start) | collective-permute-done | bytes 262176 | tf_op jit(solution)/shard_map/ppermute | solution.py:11
  67.1 3.1 %collective-permute-start.1 = (f32[3,1,128,128]{3,2,1,0:T(8,128)S(1)}, f32[3,1,128,128]{3,2,1,0:T(8,128)S(1)}, u32[]{:S(2)}, u32[]{:S(2)}) collective-permute-start(f32[3,1,128,128]{3,2,1,0:T(8,128)S(1)} %pad_maximum_fusion.1), channel_id=1, source_target_pairs={{0,64},{32,96},{64,0},{96,32},{128,192},{160,224},{192,128},{224,1... | collective-permute-start | bytes 589832 | tf_op jit(solution)/shard_map/ppermute | solution.py:11
  70.2 8.6 %collective-permute-done.1 = f32[3,1,128,128]{3,2,1,0:T(8,128)S(1)} collective-permute-done((f32[3,1,128,128]{3,2,1,0:T(8,128)S(1)}, f32[3,1,128,128]{3,2,1,0:T(8,128)S(1)}, u32[]{:S(2)}, u32[]{:S(2)}) %collective-permute-start.1) | collective-permute-done | bytes 196640 | tf_op jit(solution)/shard_map/ppermute | solution.py:11
  78.8 6.5 %collective-permute-start.2 = (f32[2,1,128,128]{3,2,1,0:T(8,128)S(1)}, f32[2,1,128,128]{3,2,1,0:T(8,128)S(1)}, u32[]{:S(2)}, u32[]{:S(2)}) collective-permute-start(f32[2,1,128,128]{3,2,1,0:T(8,128)S(1)} %pad_maximum_fusion.2), channel_id=1, source_target_pairs={{0,128},{32,160},{64,192},{96,224},{128,0},{160,32},{192,64},{224,... | collective-permute-start | bytes 393224 | tf_op jit(solution)/shard_map/ppermute | solution.py:11
  85.3 2.9 %collective-permute-done.2 = f32[2,1,128,128]{3,2,1,0:T(8,128)S(1)} collective-permute-done((f32[2,1,128,128]{3,2,1,0:T(8,128)S(1)}, f32[2,1,128,128]{3,2,1,0:T(8,128)S(1)}, u32[]{:S(2)}, u32[]{:S(2)}) %collective-permute-start.2) | collective-permute-done | bytes 131104 | tf_op jit(solution)/shard_map/ppermute | solution.py:11
  88.3 0.2 fusion.24
  88.4 0.5 broadcast.690
  89.0 0.7 reduce.24
  89.6 0.7 reshape.490
  90.3 7.9 %all-to-all-start.6 = ((bf16[32,2,1024]{2,1,0:T(2,128)(2,1)}), bf16[32,2,1024]{2,1,0:T(2,128)(2,1)S(1)}, u32[]{:S(2)}, u32[]{:S(2)}) async-start(bf16[32,2,1024]{2,1,0:T(2,128)(2,1)} %reshape.490), calls=%async_computation.6 | async-start | bytes 262144 | tf_op jit(solution)/shard_map/all_to_all | solution.py:155
  98.2 0.2 fusion.25
  98.4 0.7 reduce.23
  99.1 0.7 reshape.488
  99.8 0.3 multiply_reduce_fusion
  100.2 0.4 fusion.21
  100.6 0.7 reduce.22
  101.3 0.7 reshape.486
  102.0 4.0 %all-to-all-done.6 = bf16[32,2,1024]{2,1,0:T(2,128)(2,1)S(1)} async-done(((bf16[32,2,1024]{2,1,0:T(2,128)(2,1)}), bf16[32,2,1024]{2,1,0:T(2,128)(2,1)S(1)}, u32[]{:S(2)}, u32[]{:S(2)}) %all-to-all-start.6) | async-done | bytes 131104 | tf_op jit(solution)/shard_map/all_to_all | solution.py:155
  105.9 3.9 %all-to-all-start.5 = ((bf16[32,2,1024]{2,1,0:T(2,128)(2,1)}), bf16[32,2,1024]{2,1,0:T(2,128)(2,1)S(1)}, u32[]{:S(2)}, u32[]{:S(2)}) async-start(bf16[32,2,1024]{2,1,0:T(2,128)(2,1)} %reshape.488), calls=%async_computation.5 | async-start | bytes 262144 | tf_op jit(solution)/shard_map/all_to_all | solution.py:152
  109.9 0.6 copy-done.4
  110.6 7.0 %all-to-all-done.5 = bf16[32,2,1024]{2,1,0:T(2,128)(2,1)S(1)} async-done(((bf16[32,2,1024]{2,1,0:T(2,128)(2,1)}), bf16[32,2,1024]{2,1,0:T(2,128)(2,1)S(1)}, u32[]{:S(2)}, u32[]{:S(2)}) %all-to-all-start.5) | async-done | bytes 131104 | tf_op jit(solution)/shard_map/all_to_all | solution.py:152
  117.6 3.9 %all-to-all-start.4 = ((bf16[32,2,1024]{2,1,0:T(2,128)(2,1)}), bf16[32,2,1024]{2,1,0:T(2,128)(2,1)S(1)}, u32[]{:S(2)}, u32[]{:S(2)}) async-start(bf16[32,2,1024]{2,1,0:T(2,128)(2,1)} %reshape.486), calls=%async_computation.4 | async-start | bytes 262144 | tf_op jit(solution)/shard_map/all_to_all | solution.py:149
  121.6 0.6 copy.74
  122.4 0.7 copy.73
  123.2 0.7 copy.72
  123.9 5.3 %all-to-all-done.4 = bf16[32,2,1024]{2,1,0:T(2,128)(2,1)S(1)} async-done(((bf16[32,2,1024]{2,1,0:T(2,128)(2,1)}), bf16[32,2,1024]{2,1,0:T(2,128)(2,1)S(1)}, u32[]{:S(2)}, u32[]{:S(2)}) %all-to-all-start.4) | async-done | bytes 131104 | tf_op jit(solution)/shard_map/all_to_all | solution.py:149
  129.4 0.7 copy.71
  (46 shorter events, 1.4 us)
Async XLA Ops:
  2.2 8.7 %copy-start = (bf16[16,32,128]{2,1,0:T(8,128)(2,1)S(1)}, bf16[16,32,128]{2,1,0:T(8,128)(2,1)}, u32[]{:S(2)}) copy-start(bf16[16,32,128]{2,1,0:T(8,128)(2,1)} %param.8) | copy-start | bytes 393220
  2.2 16.3 %all-to-all-start = ((bf16[16,32,128]{2,0,1:T(8,128)(2,1)}), bf16[16,32,128]{2,0,1:T(8,128)(2,1)S(1)}, u32[]{:S(2)}, u32[]{:S(2)}) async-start(bf16[16,32,128]{2,0,1:T(8,128)(2,1)} %copy.54), calls=%async_computation | async-start | bytes 262144 | tf_op jit(solution)/shard_map/all_to_all | solution.py:113
  11.7 10.8 %copy-start.1 = (bf16[16,32,128]{2,1,0:T(8,128)(2,1)S(1)}, bf16[16,32,128]{2,1,0:T(8,128)(2,1)}, u32[]{:S(2)}) copy-start(bf16[16,32,128]{2,1,0:T(8,128)(2,1)} %param.7) | copy-start | bytes 393220
  18.6 11.6 %all-to-all-start.1 = ((bf16[16,32,128]{2,0,1:T(8,128)(2,1)}), bf16[16,32,128]{2,0,1:T(8,128)(2,1)S(1)}, u32[]{:S(2)}, u32[]{:S(2)}) async-start(bf16[16,32,128]{2,0,1:T(8,128)(2,1)} %copy.55), calls=%async_computation.1 | async-start | bytes 262144 | tf_op jit(solution)/shard_map/all_to_all | solution.py:112
  23.2 10.9 %copy-start.3 = (f32[1,13,512]{2,0,1:T(1,128)S(1)}, f32[1,13,512]{2,0,1:T(1,128)}, u32[]{:S(2)}) copy-start(f32[1,13,512]{2,0,1:T(1,128)} %param.10) | copy-start | bytes 79876
  30.2 11.6 %all-to-all-start.2 = ((bf16[16,32,128]{2,0,1:T(8,128)(2,1)}), bf16[16,32,128]{2,0,1:T(8,128)(2,1)S(1)}, u32[]{:S(2)}, u32[]{:S(2)}) async-start(bf16[16,32,128]{2,0,1:T(8,128)(2,1)} %copy.58), calls=%async_computation.2 | async-start | bytes 262144 | tf_op jit(solution)/shard_map/all_to_all | solution.py:111
  34.1 0.9 copy-start.2
  41.8 11.6 %all-to-all-start.3 = ((bf16[16,32,128]{2,0,1:T(8,128)(2,1)}), bf16[16,32,128]{2,0,1:T(8,128)(2,1)S(1)}, u32[]{:S(2)}, u32[]{:S(2)}) async-start(bf16[16,32,128]{2,0,1:T(8,128)(2,1)} %copy.62), calls=%async_computation.3 | async-start | bytes 262144 | tf_op jit(solution)/shard_map/all_to_all | solution.py:110
  58.5 2.3 %copy-start.5 = (f32[512,512]{0,1:T(8,128)S(1)}, f32[512,512]{0,1:T(8,128)}, u32[]{:S(2)}) copy-start(f32[512,512]{0,1:T(8,128)} %get-tuple-element.48) | copy-start | bytes 3145732
  59.1 7.9 %collective-permute-start = (f32[4,1,128,128]{3,2,1,0:T(8,128)S(1)}, f32[4,1,128,128]{3,2,1,0:T(8,128)S(1)}, u32[]{:S(2)}, u32[]{:S(2)}) collective-permute-start(f32[4,1,128,128]{3,2,1,0:T(8,128)S(1)} %pad_maximum_fusion), channel_id=1, source_target_pairs={{0,32},{32,0},{64,96},{96,64},{128,160},{160,128},{192,224},{224,1... | collective-permute-start | bytes 786440 | tf_op jit(solution)/shard_map/ppermute | solution.py:11
  67.1 11.7 %collective-permute-start.1 = (f32[3,1,128,128]{3,2,1,0:T(8,128)S(1)}, f32[3,1,128,128]{3,2,1,0:T(8,128)S(1)}, u32[]{:S(2)}, u32[]{:S(2)}) collective-permute-start(f32[3,1,128,128]{3,2,1,0:T(8,128)S(1)} %pad_maximum_fusion.1), channel_id=1, source_target_pairs={{0,64},{32,96},{64,0},{96,32},{128,192},{160,224},{192,128},{224,1... | collective-permute-start | bytes 589832 | tf_op jit(solution)/shard_map/ppermute | solution.py:11
  78.8 9.5 %collective-permute-start.2 = (f32[2,1,128,128]{3,2,1,0:T(8,128)S(1)}, f32[2,1,128,128]{3,2,1,0:T(8,128)S(1)}, u32[]{:S(2)}, u32[]{:S(2)}) collective-permute-start(f32[2,1,128,128]{3,2,1,0:T(8,128)S(1)} %pad_maximum_fusion.2), channel_id=1, source_target_pairs={{0,128},{32,160},{64,192},{96,224},{128,0},{160,32},{192,64},{224,... | collective-permute-start | bytes 393224 | tf_op jit(solution)/shard_map/ppermute | solution.py:11
  90.3 15.6 %all-to-all-start.6 = ((bf16[32,2,1024]{2,1,0:T(2,128)(2,1)}), bf16[32,2,1024]{2,1,0:T(2,128)(2,1)S(1)}, u32[]{:S(2)}, u32[]{:S(2)}) async-start(bf16[32,2,1024]{2,1,0:T(2,128)(2,1)} %reshape.490), calls=%async_computation.6 | async-start | bytes 262144 | tf_op jit(solution)/shard_map/all_to_all | solution.py:155
  105.9 11.6 %all-to-all-start.5 = ((bf16[32,2,1024]{2,1,0:T(2,128)(2,1)}), bf16[32,2,1024]{2,1,0:T(2,128)(2,1)S(1)}, u32[]{:S(2)}, u32[]{:S(2)}) async-start(bf16[32,2,1024]{2,1,0:T(2,128)(2,1)} %reshape.488), calls=%async_computation.5 | async-start | bytes 262144 | tf_op jit(solution)/shard_map/all_to_all | solution.py:152
  109.9 0.7 copy-start.4
  117.6 11.6 %all-to-all-start.4 = ((bf16[32,2,1024]{2,1,0:T(2,128)(2,1)}), bf16[32,2,1024]{2,1,0:T(2,128)(2,1)S(1)}, u32[]{:S(2)}, u32[]{:S(2)}) async-start(bf16[32,2,1024]{2,1,0:T(2,128)(2,1)} %reshape.486), calls=%async_computation.4 | async-start | bytes 262144 | tf_op jit(solution)/shard_map/all_to_all | solution.py:149
where the time goes:
time: 131 us; the launch traced here: 130 us
  waiting for transfers between devices  59.8 us (46%)
  starting transfers between devices  47.6 us (36%)
  local copies, waits for them, and re-layouts  11.5 us (9%)
  other arithmetic  5.47 us (4%)
  matrix products  4.65 us (4%)
    ppermute x3, waiting for transfers between devices, partner(): return lax.ppermute(value, axis, pairs)  16.3 us
    ppermute x3, starting transfers between devices, partner(): return lax.ppermute(value, axis, pairs)  11.4 us
    unnamed x29, local copies, waits for them, and re-layouts  10.4 us
    all_to_all x1, starting transfers between devices, on_device(): lax.all_to_all(out_grad, 'head', split_axis=1, concat_axis=0, tiled=True)  8.71 us
    all_to_all x1, starting transfers between devices, on_device(): lax.all_to_all(value_total.astype(jnp.bfloat16), 'head', split_axis=0, co...  7.89 us
    all_to_all x1, waiting for transfers between devices, on_device(): lax.all_to_all(queries, 'head', split_axis=1, concat_axis=0, tiled=True)  7.31 us
    all_to_all x1, waiting for transfers between devices, on_device(): lax.all_to_all(values, 'head', split_axis=1, concat_axis=0, tiled=True)  6.99 us
    all_to_all x1, waiting for transfers between devices, on_device(): lax.all_to_all(key_total.astype(jnp.bfloat16), 'head', split_axis=0, conc...  6.98 us
  transfers between devices with their start and end apart: 10, of which 10 were waited for; matrix products, arithmetic and copies ran while one was open for 8% of the time, Pallas kernels for 0%

commit v1 on v0

--- a/solution.py
+++ b/solution.py
@@ -145,6 +145,12 @@
     weight_grad = jnp.stack(
         weight_near + [weight_far[degree].T for degree in range(far_count)], axis=1
     )
+    columns_clear = lambda piece_in: jnp.concatenate(
+        jax.lax.all_to_all(
+            jnp.stack(jnp.split(piece_in, jax.lax.axis_size("head"), axis=0), axis=0), "head", 0, 0
+        ),
+        axis=1,
+    )
     query_out, key_out, value_out = (
         lax.all_to_all(
             query_total.astype(jnp.bfloat16), "head", split_axis=0, concat_axis=1, tiled=True
@@ -152,9 +158,7 @@
         lax.all_to_all(
             key_total.astype(jnp.bfloat16), "head", split_axis=0, concat_axis=1, tiled=True
         ),
-        lax.all_to_all(
-            value_total.astype(jnp.bfloat16), "head", split_axis=0, concat_axis=1, tiled=True
-        ),
+        columns_clear(value_total.astype(jnp.bfloat16)),
     )
     return (query_out, key_out, value_out, weight_grad)
 

time: 131 us -> 148 us (1.13)
  local copies, waits for them, and re-layouts: 11.5 us -> 29.7 us
    unnamed x29 -> x57, local copies, waits for them, and re-layouts: 10.4 us -> 27.9 us
  transfers between devices with their start and end apart: 10 -> 10, of which waited for: 10 -> 10; matrix products, arithmetic and copies ran while one was open for 8% -> 7% of each run, Pallas kernels for 0% -> 0%
where the time goes in v1:
time: 148 us; the launch traced here: 147 us
  waiting for transfers between devices  59.3 us (40%)
  starting transfers between devices  47.7 us (32%)
  local copies, waits for them, and re-layouts  29.7 us (20%)
  other arithmetic  4.8 us (3%)
  matrix products  4.65 us (3%)
    unnamed x57, local copies, waits for them, and re-layouts  27.9 us
    ppermute x3, waiting for transfers between devices, partner(): return lax.ppermute(value, axis, pairs)  16.3 us
    ppermute x3, starting transfers between devices, partner(): return lax.ppermute(value, axis, pairs)  11.4 us
    all_to_all x1, starting transfers between devices, on_device(): lax.all_to_all(out_grad, 'head', split_axis=1, concat_axis=0, tiled=True)  8.71 us
    all_to_all x1, starting transfers between devices, on_device(): jax.lax.all_to_all(jnp.stack(jnp.split(piece_in, jax.lax.axis_size('head'...  7.89 us
    all_to_all x1, waiting for transfers between devices, on_device(): lax.all_to_all(queries, 'head', split_axis=1, concat_axis=0, tiled=True)  7.31 us
    all_to_all x1, waiting for transfers between devices, on_device(): lax.all_to_all(values, 'head', split_axis=1, concat_axis=0, tiled=True)  6.99 us
    all_to_all x1, waiting for transfers between devices, on_device(): lax.all_to_all(out_grad, 'head', split_axis=1, concat_axis=0, tiled=True)  6.88 us
  transfers between devices with their start and end apart: 10, of which 10 were waited for; matrix products, arithmetic and copies ran while one was open for 7% of the time, Pallas kernels for 0%

profile of v1, /device:TPU:1, one launch (start us, length us, event | category | flops | bytes accessed | tf_op | source)
XLA Modules:
  0.0 147.2 jit_solution(2801957886462717193)
XLA Ops:
  0.6 1.6 %copy.53 = bf16[16,32,128]{2,0,1:T(8,128)(2,1)} copy(bf16[16,32,128]{2,1,0:T(8,128)(2,1)} %param.9) | data formatting | bytes 262144 | tf_op args[3]
  2.2 8.7 %all-to-all-start = ((bf16[16,32,128]{2,0,1:T(8,128)(2,1)}), bf16[16,32,128]{2,0,1:T(8,128)(2,1)S(1)}, u32[]{:S(2)}, u32[]{:S(2)}) async-start(bf16[16,32,128]{2,0,1:T(8,128)(2,1)} %copy.53), calls=%async_computation | async-start | bytes 262144 | tf_op jit(solution)/shard_map/all_to_all | solution.py:113
  11.0 0.7 copy.54
  11.7 6.9 %all-to-all-done = bf16[16,32,128]{2,0,1:T(8,128)(2,1)S(1)} async-done(((bf16[16,32,128]{2,0,1:T(8,128)(2,1)}), bf16[16,32,128]{2,0,1:T(8,128)(2,1)S(1)}, u32[]{:S(2)}, u32[]{:S(2)}) %all-to-all-start) | async-done | bytes 131104 | tf_op jit(solution)/shard_map/all_to_all | solution.py:113
  18.6 3.9 %all-to-all-start.1 = ((bf16[16,32,128]{2,0,1:T(8,128)(2,1)}), bf16[16,32,128]{2,0,1:T(8,128)(2,1)S(1)}, u32[]{:S(2)}, u32[]{:S(2)}) async-start(bf16[16,32,128]{2,0,1:T(8,128)(2,1)} %copy.54), calls=%async_computation.1 | async-start | bytes 262144 | tf_op jit(solution)/shard_map/all_to_all | solution.py:112
  22.5 0.7 copy.57
  23.2 7.0 %all-to-all-done.1 = bf16[16,32,128]{2,0,1:T(8,128)(2,1)S(1)} async-done(((bf16[16,32,128]{2,0,1:T(8,128)(2,1)}), bf16[16,32,128]{2,0,1:T(8,128)(2,1)S(1)}, u32[]{:S(2)}, u32[]{:S(2)}) %all-to-all-start.1) | async-done | bytes 131104 | tf_op jit(solution)/shard_map/all_to_all | solution.py:112
  30.2 3.9 %all-to-all-start.2 = ((bf16[16,32,128]{2,0,1:T(8,128)(2,1)}), bf16[16,32,128]{2,0,1:T(8,128)(2,1)S(1)}, u32[]{:S(2)}, u32[]{:S(2)}) async-start(bf16[16,32,128]{2,0,1:T(8,128)(2,1)} %copy.57), calls=%async_computation.2 | async-start | bytes 262144 | tf_op jit(solution)/shard_map/all_to_all | solution.py:111
  34.2 0.8 copy-done.2
  35.1 0.7 copy.61
  35.9 6.0 %all-to-all-done.2 = bf16[16,32,128]{2,0,1:T(8,128)(2,1)S(1)} async-done(((bf16[16,32,128]{2,0,1:T(8,128)(2,1)}), bf16[16,32,128]{2,0,1:T(8,128)(2,1)S(1)}, u32[]{:S(2)}, u32[]{:S(2)}) %all-to-all-start.2) | async-done | bytes 131104 | tf_op jit(solution)/shard_map/all_to_all | solution.py:111
  41.8 3.9 %all-to-all-start.3 = ((bf16[16,32,128]{2,0,1:T(8,128)(2,1)}), bf16[16,32,128]{2,0,1:T(8,128)(2,1)S(1)}, u32[]{:S(2)}, u32[]{:S(2)}) async-start(bf16[16,32,128]{2,0,1:T(8,128)(2,1)} %copy.61), calls=%async_computation.3 | async-start | bytes 262144 | tf_op jit(solution)/shard_map/all_to_all | solution.py:110
  46.2 7.3 %all-to-all-done.3 = bf16[16,32,128]{2,0,1:T(8,128)(2,1)S(1)} async-done(((bf16[16,32,128]{2,0,1:T(8,128)(2,1)}), bf16[16,32,128]{2,0,1:T(8,128)(2,1)S(1)}, u32[]{:S(2)}, u32[]{:S(2)}) %all-to-all-start.3) | async-done | bytes 131104 | tf_op jit(solution)/shard_map/all_to_all | solution.py:110
  53.5 1.7 %fusion.9 = (f32[512,512]{0,1:T(8,128)S(1)}, bf16[512,512]{0,1:T(8,128)(2,1)S(1)}, f32[512,512]{0,1:T(8,128)}) fusion(f32[512,512]{0,1:T(8,128)S(1)} %fusion.61, f32[512]{0:T(512)S(1)} %bitcast.310, f32[512]{0:T(512)S(1)} %bitcast.312, f32[512]{0:T(512)S(1)} %bitcast.314, f32[512]{0:T(512)S(1)} %bitcast.316, f32[512]{0:T(512)S(1)} %bitcast.318, ...), kind=kOutput, calls=%fused_computation.11 | convolution fusion | flops 83361792 | bytes 3952640 | tf_op jit(solution)/shard_map/thd,shd->hts/dot_general | solution.py:82
  55.2 3.1 %select_reduce_fusion = (f32[512]{0:T(512)S(1)}, f32[512]{0:T(512)S(1)}, f32[512]{0:T(512)S(1)}, f32[512]{0:T(512)S(1)}, f32[512]{0:T(512)S(1)}, /*index=5*/f32[...) fusion(f32[512,512]{0,1:T(8,128)S(1)} %get-tuple-element.32), kind=kLoop, calls=%fused_computation.35 | loop fusion | flops 17820672 | bytes 1069056 | tf_op jit(solution)/shard_map/reduce_sum | solution.py:91
  59.1 1.7 %collective-permute-start = (f32[4,1,128,128]{3,2,1,0:T(8,128)S(1)}, f32[4,1,128,128]{3,2,1,0:T(8,128)S(1)}, u32[]{:S(2)}, u32[]{:S(2)}) collective-permute-start(f32[4,1,128,128]{3,2,1,0:T(8,128)S(1)} %pad_maximum_fusion), channel_id=1, source_target_pairs={{0,32},{32,0},{64,96},{96,64},{128,160},{160,128},{192,224},{224,1... | collective-permute-start | bytes 786440 | tf_op jit(solution)/shard_map/ppermute | solution.py:11
  60.8 0.8 convolution_bitcast_fusion.1
  62.2 4.8 %collective-permute-done = f32[4,1,128,128]{3,2,1,0:T(8,128)S(1)} collective-permute-done((f32[4,1,128,128]{3,2,1,0:T(8,128)S(1)}, f32[4,1,128,128]{3,2,1,0:T(8,128)S(1)}, u32[]{:S(2)}, u32[]{:S(2)}) %collective-permute-start) | collective-permute-done | bytes 262176 | tf_op jit(solution)/shard_map/ppermute | solution.py:11
  67.1 3.1 %collective-permute-start.1 = (f32[3,1,128,128]{3,2,1,0:T(8,128)S(1)}, f32[3,1,128,128]{3,2,1,0:T(8,128)S(1)}, u32[]{:S(2)}, u32[]{:S(2)}) collective-permute-start(f32[3,1,128,128]{3,2,1,0:T(8,128)S(1)} %pad_maximum_fusion.1), channel_id=1, source_target_pairs={{0,64},{32,96},{64,0},{96,32},{128,192},{160,224},{192,128},{224,1... | collective-permute-start | bytes 589832 | tf_op jit(solution)/shard_map/ppermute | solution.py:11
  70.2 8.6 %collective-permute-done.1 = f32[3,1,128,128]{3,2,1,0:T(8,128)S(1)} collective-permute-done((f32[3,1,128,128]{3,2,1,0:T(8,128)S(1)}, f32[3,1,128,128]{3,2,1,0:T(8,128)S(1)}, u32[]{:S(2)}, u32[]{:S(2)}) %collective-permute-start.1) | collective-permute-done | bytes 196640 | tf_op jit(solution)/shard_map/ppermute | solution.py:11
  78.8 6.5 %collective-permute-start.2 = (f32[2,1,128,128]{3,2,1,0:T(8,128)S(1)}, f32[2,1,128,128]{3,2,1,0:T(8,128)S(1)}, u32[]{:S(2)}, u32[]{:S(2)}) collective-permute-start(f32[2,1,128,128]{3,2,1,0:T(8,128)S(1)} %pad_maximum_fusion.2), channel_id=1, source_target_pairs={{0,128},{32,160},{64,192},{96,224},{128,0},{160,32},{192,64},{224,... | collective-permute-start | bytes 393224 | tf_op jit(solution)/shard_map/ppermute | solution.py:11
  85.3 2.9 %collective-permute-done.2 = f32[2,1,128,128]{3,2,1,0:T(8,128)S(1)} collective-permute-done((f32[2,1,128,128]{3,2,1,0:T(8,128)S(1)}, f32[2,1,128,128]{3,2,1,0:T(8,128)S(1)}, u32[]{:S(2)}, u32[]{:S(2)}) %collective-permute-start.2) | collective-permute-done | bytes 131104 | tf_op jit(solution)/shard_map/ppermute | solution.py:11
  88.5 0.6 constant_dynamic-update-slice_fusion.31
  89.1 0.6 constant_dynamic-update-slice_fusion.30
  90.2 0.6 constant_dynamic-update-slice_fusion.28
  90.8 0.6 constant_dynamic-update-slice_fusion.27
  91.4 0.6 constant_dynamic-update-slice_fusion.26
  92.0 0.6 constant_dynamic-update-slice_fusion.25
  92.6 0.6 constant_dynamic-update-slice_fusion.24
  93.2 0.6 constant_dynamic-update-slice_fusion.23
  93.8 0.6 constant_dynamic-update-slice_fusion.22
  94.4 0.6 constant_dynamic-update-slice_fusion.21
  95.0 0.6 constant_dynamic-update-slice_fusion.20
  107.5 7.9 %all-to-all-start.6 = ((bf16[32,16,1,128]{3,1,2,0:T(8,128)(2,1)}), bf16[32,16,1,128]{3,1,2,0:T(8,128)(2,1)S(1)}, u32[]{:S(2)}, u32[]{:S(2)}) async-start(bf16[32,16,1,128]{3,1,2,0:T(8,128)(2,1)} %constant_dynamic-update-slice_fusion), calls=%async_computation.6 | async-start | bytes 262144 | tf_op jit(solution)/shard_map/all_to_all | solution.py:149
  116.1 0.7 reduce.23
  116.7 0.7 reshape.496
  118.2 0.7 reduce.22
  118.9 0.7 reshape.494
  119.6 3.5 %all-to-all-done.6 = bf16[32,16,1,128]{3,1,2,0:T(8,128)(2,1)S(1)} async-done(((bf16[32,16,1,128]{3,1,2,0:T(8,128)(2,1)}), bf16[32,16,1,128]{3,1,2,0:T(8,128)(2,1)S(1)}, u32[]{:S(2)}, u32[]{:S(2)}) %all-to-all-start.6) | async-done | bytes 131104 | tf_op jit(solution)/shard_map/all_to_all | solution.py:149
  123.1 4.0 %all-to-all-start.5 = ((bf16[32,2,1024]{2,1,0:T(2,128)(2,1)}), bf16[32,2,1024]{2,1,0:T(2,128)(2,1)S(1)}, u32[]{:S(2)}, u32[]{:S(2)}) async-start(bf16[32,2,1024]{2,1,0:T(2,128)(2,1)} %reshape.496), calls=%async_computation.5 | async-start | bytes 262144 | tf_op jit(solution)/shard_map/all_to_all | solution.py:158
  127.1 0.6 copy-done.4
  127.8 6.9 %all-to-all-done.5 = bf16[32,2,1024]{2,1,0:T(2,128)(2,1)S(1)} async-done(((bf16[32,2,1024]{2,1,0:T(2,128)(2,1)}), bf16[32,2,1024]{2,1,0:T(2,128)(2,1)S(1)}, u32[]{:S(2)}, u32[]{:S(2)}) %all-to-all-start.5) | async-done | bytes 131104 | tf_op jit(solution)/shard_map/all_to_all | solution.py:158
  134.7 3.9 %all-to-all-start.4 = ((bf16[32,2,1024]{2,1,0:T(2,128)(2,1)}), bf16[32,2,1024]{2,1,0:T(2,128)(2,1)S(1)}, u32[]{:S(2)}, u32[]{:S(2)}) async-start(bf16[32,2,1024]{2,1,0:T(2,128)(2,1)} %reshape.494), calls=%async_computation.4 | async-start | bytes 262144 | tf_op jit(solution)/shard_map/all_to_all | solution.py:155
  138.7 0.6 copy.72
  139.4 0.7 copy.71
  140.2 0.7 copy.70
  140.9 5.5 %all-to-all-done.4 = bf16[32,2,1024]{2,1,0:T(2,128)(2,1)S(1)} async-done(((bf16[32,2,1024]{2,1,0:T(2,128)(2,1)}), bf16[32,2,1024]{2,1,0:T(2,128)(2,1)S(1)}, u32[]{:S(2)}, u32[]{:S(2)}) %all-to-all-start.4) | async-done | bytes 131104 | tf_op jit(solution)/shard_map/all_to_all | solution.py:155
  146.5 0.7 copy.69
  (74 shorter events, 16.3 us)
Async XLA Ops:
  2.2 8.7 %copy-start = (bf16[16,32,128]{2,1,0:T(8,128)(2,1)S(1)}, bf16[16,32,128]{2,1,0:T(8,128)(2,1)}, u32[]{:S(2)}) copy-start(bf16[16,32,128]{2,1,0:T(8,128)(2,1)} %param.8) | copy-start | bytes 393220
  2.2 16.3 %all-to-all-start = ((bf16[16,32,128]{2,0,1:T(8,128)(2,1)}), bf16[16,32,128]{2,0,1:T(8,128)(2,1)S(1)}, u32[]{:S(2)}, u32[]{:S(2)}) async-start(bf16[16,32,128]{2,0,1:T(8,128)(2,1)} %copy.53), calls=%async_computation | async-start | bytes 262144 | tf_op jit(solution)/shard_map/all_to_all | solution.py:113
  11.7 10.8 %copy-start.1 = (bf16[16,32,128]{2,1,0:T(8,128)(2,1)S(1)}, bf16[16,32,128]{2,1,0:T(8,128)(2,1)}, u32[]{:S(2)}) copy-start(bf16[16,32,128]{2,1,0:T(8,128)(2,1)} %param.7) | copy-start | bytes 393220
  18.6 11.6 %all-to-all-start.1 = ((bf16[16,32,128]{2,0,1:T(8,128)(2,1)}), bf16[16,32,128]{2,0,1:T(8,128)(2,1)S(1)}, u32[]{:S(2)}, u32[]{:S(2)}) async-start(bf16[16,32,128]{2,0,1:T(8,128)(2,1)} %copy.54), calls=%async_computation.1 | async-start | bytes 262144 | tf_op jit(solution)/shard_map/all_to_all | solution.py:112
  23.2 10.9 %copy-start.3 = (f32[1,13,512]{2,0,1:T(1,128)S(1)}, f32[1,13,512]{2,0,1:T(1,128)}, u32[]{:S(2)}) copy-start(f32[1,13,512]{2,0,1:T(1,128)} %param.10) | copy-start | bytes 79876
  30.2 11.6 %all-to-all-start.2 = ((bf16[16,32,128]{2,0,1:T(8,128)(2,1)}), bf16[16,32,128]{2,0,1:T(8,128)(2,1)S(1)}, u32[]{:S(2)}, u32[]{:S(2)}) async-start(bf16[16,32,128]{2,0,1:T(8,128)(2,1)} %copy.57), calls=%async_computation.2 | async-start | bytes 262144 | tf_op jit(solution)/shard_map/all_to_all | solution.py:111
  34.1 0.9 copy-start.2
  41.8 11.6 %all-to-all-start.3 = ((bf16[16,32,128]{2,0,1:T(8,128)(2,1)}), bf16[16,32,128]{2,0,1:T(8,128)(2,1)S(1)}, u32[]{:S(2)}, u32[]{:S(2)}) async-start(bf16[16,32,128]{2,0,1:T(8,128)(2,1)} %copy.61), calls=%async_computation.3 | async-start | bytes 262144 | tf_op jit(solution)/shard_map/all_to_all | solution.py:110
  58.5 2.3 %copy-start.5 = (f32[512,512]{0,1:T(8,128)S(1)}, f32[512,512]{0,1:T(8,128)}, u32[]{:S(2)}) copy-start(f32[512,512]{0,1:T(8,128)} %get-tuple-element.52) | copy-start | bytes 3145732
  59.1 7.9 %collective-permute-start = (f32[4,1,128,128]{3,2,1,0:T(8,128)S(1)}, f32[4,1,128,128]{3,2,1,0:T(8,128)S(1)}, u32[]{:S(2)}, u32[]{:S(2)}) collective-permute-start(f32[4,1,128,128]{3,2,1,0:T(8,128)S(1)} %pad_maximum_fusion), channel_id=1, source_target_pairs={{0,32},{32,0},{64,96},{96,64},{128,160},{160,128},{192,224},{224,1... | collective-permute-start | bytes 786440 | tf_op jit(solution)/shard_map/ppermute | solution.py:11
  67.1 11.7 %collective-permute-start.1 = (f32[3,1,128,128]{3,2,1,0:T(8,128)S(1)}, f32[3,1,128,128]{3,2,1,0:T(8,128)S(1)}, u32[]{:S(2)}, u32[]{:S(2)}) collective-permute-start(f32[3,1,128,128]{3,2,1,0:T(8,128)S(1)} %pad_maximum_fusion.1), channel_id=1, source_target_pairs={{0,64},{32,96},{64,0},{96,32},{128,192},{160,224},{192,128},{224,1... | collective-permute-start | bytes 589832 | tf_op jit(solution)/shard_map/ppermute | solution.py:11
  78.8 9.5 %collective-permute-start.2 = (f32[2,1,128,128]{3,2,1,0:T(8,128)S(1)}, f32[2,1,128,128]{3,2,1,0:T(8,128)S(1)}, u32[]{:S(2)}, u32[]{:S(2)}) collective-permute-start(f32[2,1,128,128]{3,2,1,0:T(8,128)S(1)} %pad_maximum_fusion.2), channel_id=1, source_target_pairs={{0,128},{32,160},{64,192},{96,224},{128,0},{160,32},{192,64},{224,... | collective-permute-start | bytes 393224 | tf_op jit(solution)/shard_map/ppermute | solution.py:11
  107.5 15.6 %all-to-all-start.6 = ((bf16[32,16,1,128]{3,1,2,0:T(8,128)(2,1)}), bf16[32,16,1,128]{3,1,2,0:T(8,128)(2,1)S(1)}, u32[]{:S(2)}, u32[]{:S(2)}) async-start(bf16[32,16,1,128]{3,1,2,0:T(8,128)(2,1)} %constant_dynamic-update-slice_fusion), calls=%async_computation.6 | async-start | bytes 262144 | tf_op jit(solution)/shard_map/all_to_all | solution.py:149
  123.1 11.6 %all-to-all-start.5 = ((bf16[32,2,1024]{2,1,0:T(2,128)(2,1)}), bf16[32,2,1024]{2,1,0:T(2,128)(2,1)S(1)}, u32[]{:S(2)}, u32[]{:S(2)}) async-start(bf16[32,2,1024]{2,1,0:T(2,128)(2,1)} %reshape.496), calls=%async_computation.5 | async-start | bytes 262144 | tf_op jit(solution)/shard_map/all_to_all | solution.py:158
  127.1 0.7 copy-start.4
  134.7 11.6 %all-to-all-start.4 = ((bf16[32,2,1024]{2,1,0:T(2,128)(2,1)}), bf16[32,2,1024]{2,1,0:T(2,128)(2,1)S(1)}, u32[]{:S(2)}, u32[]{:S(2)}) async-start(bf16[32,2,1024]{2,1,0:T(2,128)(2,1)} %reshape.494), calls=%async_computation.4 | async-start | bytes 262144 | tf_op jit(solution)/shard_map/all_to_all | solution.py:155
